TPU v7x, 32 devices: a whole 2x2x4 slice. The times are simulated.
32 devices in a mesh: gx: 8 (over z, x), gy: 4 (over y, core).
Axes of the slice: x: 2, y: 2, z: 4, core: 2. Of those that a mesh axis runs over, the one named last changes fastest.
Arguments:
- mean_field: float32 [16, 128, 1024], P(None, 'gx', 'gy'), may hold values from -6 to 6
- mode_fields: float32 [16, 16, 128, 1024], P(None, None, 'gx', 'gy'), may hold values from -6 to 6
- velocity_east: float32 [16, 128, 1024], P(None, 'gx', 'gy'), may hold values from -6 to 6
- velocity_north: float32 [16, 128, 1024], P(None, 'gx', 'gy'), may hold values from -6 to 6
- flag_east: int32 [16, 128, 1024], P(None, 'gx', 'gy'), may hold values 0 or 1
- flag_north: int32 [16, 128, 1024], P(None, 'gx', 'gy'), may hold values 0 or 1
- ocean_mask: int32 [16, 128, 1024], P(None, 'gx', 'gy'), may hold values 0 or 1
Outputs:
- mean_next: float32 [16, 128, 1024], P(None, 'gx', 'gy')
- modes_next: float32 [16, 16, 128, 1024], P(None, None, 'gx', 'gy')
- factor: float32 [16, 16], replicated
Inputs may be any that keep to these rules, and one draw needn't show every extreme that they name: `flag_east`: 1 takes the five-point upwind value biased to the cell of lower index beside the face, 0 the one biased to the higher. `flag_north`: as for the first dimension. `ocean_mask`: 1 marks ocean, 0 land.
All inputs are finite; a program needn't handle non-finite values. No bound on the sum of `flag_east` or of `flag_north` or of `ocean_mask` on one device may be relied on, other than what follows from the above.
Results may differ from a plain program's by a relative error of at most 0.0003.
Values sent between devices are 32-bit elements; how exact they have to be, the bound alone decides.
A program may use at most 128 MiB of HBM per device.

v0:
```python
import functools

import jax
import jax.numpy as jnp
from jax import lax
from jax.experimental import pallas as pl
from jax.experimental.pallas import tpu as pltpu
from jax.sharding import PartitionSpec as P


time_step = 0.1
horiz_diff = 0.05
vert_diff = 0.2
HALO = 3
LANES = 128
SUB = 8
HIGHEST = lax.Precision.HIGHEST
MESH = pl.DeviceIdType.MESH


def layers_kernel(modes, mean, east, flag, mask, x_last, x_first, aux_last, aux_first):
    count, levels, size_x, _ = modes.shape

    @pl.when(pl.program_id(0) == 0)
    def _():
        for j in range(HALO):
            aux_last[j] = mean[:, size_x - HALO + j, :]
            aux_first[j] = mean[:, j, :]
        aux_last[HALO] = mask[:, size_x - 1, :].astype(jnp.float32)
        aux_first[HALO] = mask[:, 0, :].astype(jnp.float32)
        aux_last[HALO + 1] = east[:, size_x - 1, :]
        aux_last[HALO + 2] = flag[:, size_x - 1, :].astype(jnp.float32)

    for k in range(levels):
        for f in range(count):
            x_last[k, HALO * f : HALO * (f + 1), :] = modes[f, k, size_x - HALO :, :]
            x_first[k, HALO * f : HALO * (f + 1), :] = modes[f, k, :HALO, :]


def columns_kernel(after_layers, modes, mean, north, flag_north, mask, y_last, y_first):
    count, levels, size_x, size_y = modes.shape
    lane = lax.broadcasted_iota(jnp.int32, (size_x, LANES), 1)

    def put(packed, tile, source_lane, target_lane, width):
        moved = pltpu.roll(tile, (target_lane - source_lane) % LANES, 1)
        return jnp.where((lane >= target_lane) & (lane < target_lane + width), moved, packed)

    for k in range(levels):
        mask_value = mask[k].astype(jnp.float32)
        last = jnp.zeros((size_x, LANES), jnp.float32)
        first = jnp.zeros((size_x, LANES), jnp.float32)
        for f in range(count):
            last = put(last, modes[f, k, :, size_y - LANES :], LANES - HALO, HALO * f, HALO)
            first = put(first, modes[f, k, :, :LANES], 0, HALO * f, HALO)
        base = HALO * count
        last = put(last, mean[k, :, size_y - LANES :], LANES - HALO, base, HALO)
        first = put(first, mean[k, :, :LANES], 0, base, HALO)
        base += HALO
        last = put(last, mask_value[:, size_y - LANES :], LANES - 1, base, 1)
        first = put(first, mask_value[:, :LANES], 0, base, 1)
        last = put(last, north[k, :, size_y - LANES :], LANES - 1, base + 1, 1)
        last = put(last, flag_north[k, :, size_y - LANES :].astype(jnp.float32), LANES - 1, base + 2, 1)
        y_last[k] = last
        y_first[k] = first


def interior_kernel(field, before, after, *rest):
    coefs_x, coefs_y, centre, vertical, out = rest[:6], rest[6:12], rest[12], rest[13], rest[14]
    group, levels, size_x, size_y = field.shape
    f0 = pl.program_id(0) * group
    lane = lax.broadcasted_iota(jnp.int32, (size_x, LANES), 1)
    tiles = size_y // LANES
    shifts = (-3, -2, -1, 1, 2, 3)

    def level(k, carry):
        above = jnp.minimum(k + 1, levels - 1)
        below = jnp.maximum(k - 1, 0)
        for g in range(group):
            f = f0 + g
            left = pltpu.roll(before[k], LANES - HALO - HALO * f, 1)
            right = pltpu.roll(after[k], LANES - HALO * f, 1)
            row = [left] + [field[g, k, :, t * LANES : (t + 1) * LANES] for t in range(tiles)] + [right]
            for t in range(tiles):
                cut = slice(t * LANES, (t + 1) * LANES)
                c = row[t + 1]
                total = centre[k, :, cut] * c + vertical[k, :, cut] * (field[g, above, :, cut] + field[g, below, :, cut])
                for i, s in enumerate(shifts):
                    total += coefs_x[i][k, :, cut] * pltpu.roll(c, (-s) % size_x, 0)
                    if s < 0:
                        mixed = jnp.where(lane >= LANES + s, row[t], c)
                    else:
                        mixed = jnp.where(lane < s, row[t + 2], c)
                    total += coefs_y[i][k, :, cut] * pltpu.roll(mixed, (-s) % LANES, 1)
                out[g, k, :, cut] = total
        return carry

    lax.fori_loop(0, levels, level, 0, unroll=2)


def gram_kernel(
    nx, ny, modes, partial, low, high, l3, l2, l1, h1, h2, h3, tend, gram,
    low_rows, high_rows, total, mine, gathered, send_sem, recv_sem,
):
    z = pl.program_id(0)
    me = lax.axis_index("gx") * ny + lax.axis_index("gy")
    devices = nx * ny
    barrier = pltpu.get_barrier_semaphore()
    count, levels, size_x, size_y = modes.shape

    def place(k):
        other = lax.rem(me + k, devices)
        return other, (other // ny, lax.rem(other, ny))

    def copy(k, slot):
        return pltpu.make_async_remote_copy(
            src_ref=mine,
            dst_ref=gathered.at[slot],
            send_sem=send_sem.at[k],
            recv_sem=recv_sem.at[slot],
            device_id=place(k)[1],
            device_id_type=MESH,
        )

    rows = low.shape[1]
    wide = 2 * count * SUB

    @pl.when(z == 0)
    def _():
        def greet(k, carry):
            pl.semaphore_signal(barrier, inc=1, device_id=place(k)[1], device_id_type=MESH)
            return carry

        lax.fori_loop(1, devices, greet, 0)
        low_rows[...] = jnp.zeros_like(low_rows)
        high_rows[...] = jnp.zeros_like(high_rows)
        total[...] = jnp.zeros_like(total)

    for k in range(levels):
        low_rows[k, SUB : SUB + rows, :] = low[k]
        high_rows[k, SUB : SUB + rows, :] = high[k]
        for f in range(count):
            at = SUB + HALO * f
            if size_x > 2 * SUB:
                tend[f, k] = partial[f, k]
            tend[f, k, :SUB, :] = partial[f, k, :SUB, :] + (
                l3[k] * low_rows[k, at : at + SUB, :]
                + l2[k] * low_rows[k, at + 1 : at + 1 + SUB, :]
                + l1[k] * low_rows[k, at + 2 : at + 2 + SUB, :]
            )
            base = tend if size_x == SUB else partial
            tend[f, k, size_x - SUB :, :] = base[f, k, size_x - SUB :, :] + (
                h1[k] * high_rows[k, at - 7 : at - 7 + SUB, :]
                + h2[k] * high_rows[k, at - 6 : at - 6 + SUB, :]
                + h3[k] * high_rows[k, at - 5 : at - 5 + SUB, :]
            )
    contract = (((1,), (1,)), ((), ()))
    for part in range(size_x // SUB):
        cut = slice(part * SUB, (part + 1) * SUB)
        both = jnp.concatenate(
            [
                jnp.concatenate([ref[:, k, cut, :].reshape(count * SUB, size_y) for k in range(levels)], axis=1)
                for ref in (modes, tend)
            ],
            axis=0,
        )
        coarse = both.astype(jnp.bfloat16)
        fine = (both - coarse.astype(jnp.float32)).astype(jnp.bfloat16)
        total[...] += lax.dot_general(
            jnp.concatenate([coarse, fine], axis=0), coarse, contract, preferred_element_type=jnp.float32
        )

    @pl.when(z == pl.num_programs(0) - 1)
    def _():
        row = lax.broadcasted_iota(jnp.int32, (wide, wide), 0)
        col = lax.broadcasted_iota(jnp.int32, (wide, wide), 1)
        kept = (row % SUB) == (col % SUB)
        cross = total[wide:, :]
        summed = jnp.where(kept, total[:wide, :] + cross + cross.T, 0.0)
        pick = (
            lax.broadcasted_iota(jnp.int32, (2 * count, wide), 1) // SUB
            == lax.broadcasted_iota(jnp.int32, (2 * count, wide), 0)
        ).astype(jnp.float32)
        width = gram.shape[1]
        spread = (
            lax.broadcasted_iota(jnp.int32, (wide, width), 0) // SUB
            == lax.broadcasted_iota(jnp.int32, (wide, width), 1) % (2 * count)
        ).astype(jnp.float32)
        half = jnp.dot(pick, summed, precision=HIGHEST, preferred_element_type=jnp.float32)
        full = jnp.dot(half, spread, precision=HIGHEST, preferred_element_type=jnp.float32)
        height = gram.shape[0]
        block = lax.broadcasted_iota(jnp.int32, gram.shape, 1) // (2 * count)
        packed = full[:height]
        for b in range(1, 2 * count // height):
            packed = jnp.where(block == b, full[b * height : (b + 1) * height], packed)
        mine[...] = packed
        gathered[me] = packed
        pl.semaphore_wait(barrier, devices - 1)

        def send(k, carry):
            copy(k, me).start()
            return carry

        def arrive(k, carry):
            copy(k, place(k)[0]).wait_recv()
            return carry

        def sent(k, carry):
            copy(k, me).wait_send()
            return carry

        def add(k, value):
            return value + gathered[k]

        lax.fori_loop(1, devices, send, 0)
        lax.fori_loop(1, devices, arrive, 0)
        gram[...] = lax.fori_loop(1, devices, add, gathered[0])
        lax.fori_loop(1, devices, sent, 0)


def solve(packed, count, cells):
    two = 2 * count
    height, width = packed.shape
    block = lax.broadcasted_iota(jnp.int32, packed.shape, 1) // two
    stacked = jnp.concatenate([jnp.where(block == b, packed, 0.0) for b in range(two // height)], axis=0)
    fold = (
        lax.broadcasted_iota(jnp.int32, (width, two), 0) % two == lax.broadcasted_iota(jnp.int32, (width, two), 1)
    ).astype(jnp.float32)
    total = jnp.dot(stacked, fold, precision=HIGHEST, preferred_element_type=jnp.float32) / cells
    row = lax.broadcasted_iota(jnp.int32, (count, two), 0)
    col = lax.broadcasted_iota(jnp.int32, (count, two), 1)
    contract = (((1,), (1,)), ((), ()))
    update = jnp.where(
        col < count,
        jnp.where(col == row, 1.0, 0.0) - time_step * total[count:, :],
        jnp.where(col == row + count, time_step, 0.0),
    )
    padding = jnp.zeros((count, two), jnp.float32)
    halfway = jnp.dot(update, total, precision=HIGHEST, preferred_element_type=jnp.float32)
    work = lax.dot_general(
        halfway,
        jnp.concatenate([update, padding], axis=0),
        contract,
        precision=HIGHEST,
        preferred_element_type=jnp.float32,
    )
    work = work + jnp.where(col == row + count, 1.0, 0.0)
    for j in range(count):
        column = jnp.broadcast_to(work[:, j : j + 1], (count, two))
        scale = lax.rsqrt(column[j : j + 1, :])
        pivot_row = work[j : j + 1, :] * scale
        work = jnp.where(row > j, work - (column * scale) * pivot_row, jnp.where(row == j, pivot_row, work))
    factor = jnp.where(col >= row, work, 0.0)[:, :count]
    inverse = jnp.where(col >= count, work, 0.0)
    mix = jnp.dot(
        inverse,
        jnp.concatenate([padding, update], axis=0),
        precision=HIGHEST,
        preferred_element_type=jnp.float32,
    )
    return factor, mix


def combine_kernel(cells, packed, modes, tend, out, factor, weights):
    z = pl.program_id(0)
    count, levels, size_x, size_y = modes.shape
    tall, wide = count * SUB, 2 * count * SUB

    @pl.when(z == 0)
    def _():
        factor[...], mix = solve(packed[...], count, cells)
        spread = (
            lax.broadcasted_iota(jnp.int32, (tall, count), 0) // SUB
            == lax.broadcasted_iota(jnp.int32, (tall, count), 1)
        ).astype(jnp.float32)
        along = (
            lax.broadcasted_iota(jnp.int32, (2 * count, wide), 1) // SUB
            == lax.broadcasted_iota(jnp.int32, (2 * count, wide), 0)
        ).astype(jnp.float32)
        whole = jnp.dot(
            jnp.dot(spread, mix, precision=HIGHEST, preferred_element_type=jnp.float32),
            along,
            precision=HIGHEST,
            preferred_element_type=jnp.float32,
        )
        row = lax.broadcasted_iota(jnp.int32, (tall, wide), 0)
        col = lax.broadcasted_iota(jnp.int32, (tall, wide), 1)
        whole = jnp.where((row % SUB) == (col % SUB), whole, 0.0)
        coarse = whole.astype(jnp.bfloat16)
        weights[:tall, :] = coarse
        weights[tall:, :] = (whole - coarse.astype(jnp.float32)).astype(jnp.bfloat16)

    for k in range(levels):
        for part in range(size_x // SUB):
            cut = slice(part * SUB, (part + 1) * SUB)
            both = jnp.concatenate(
                [modes[:, k, cut, :].reshape(count * SUB, size_y), tend[:, k, cut, :].reshape(count * SUB, size_y)],
                axis=0,
            )
            coarse = both.astype(jnp.bfloat16)
            fine = (both - coarse.astype(jnp.float32)).astype(jnp.bfloat16)
            main = jnp.dot(weights[...], coarse, preferred_element_type=jnp.float32)
            result = main[:tall] + (
                main[tall:] + jnp.dot(weights[:tall, :], fine, preferred_element_type=jnp.float32)
            )
            out[:, k, cut, :] = result.reshape(count, SUB, size_y)


def divisor(size, most):
    return max(d for d in range(1, most + 1) if size % d == 0)


def stencil(pos, neg, openness, cells, axis):
    face = {
        -2: openness * (2.0 * pos) / 60.0,
        -1: openness * (-13.0 * pos - 3.0 * neg) / 60.0,
        0: openness * ((47.0 * pos + 27.0 * neg) / 60.0 + horiz_diff),
        1: openness * ((27.0 * pos + 47.0 * neg) / 60.0 - horiz_diff),
        2: openness * (-3.0 * pos - 13.0 * neg) / 60.0,
        3: openness * (2.0 * neg) / 60.0,
    }
    size = cells.shape[axis]
    result = {}
    for s in range(-3, 4):
        value = 0.0
        if s + 1 in face:
            value = value + lax.slice_in_dim(face[s + 1], 0, size, axis=axis)
        if s in face:
            value = value - lax.slice_in_dim(face[s], 1, size + 1, axis=axis)
        result[s] = cells * value
    return result


def section(mean_field, mode_fields, velocity_east, velocity_north, flag_east, flag_north, ocean_mask):
    count, levels, size_x, size_y = mode_fields.shape
    nx, ny = lax.axis_size("gx"), lax.axis_size("gy")
    f32 = jnp.float32

    def up(value, axis):
        return lax.ppermute(value, axis, [(i, i + 1) for i in range(lax.axis_size(axis) - 1)])

    def down(value, axis):
        return lax.ppermute(value, axis, [(i + 1, i) for i in range(lax.axis_size(axis) - 1)])

    wet = ocean_mask.astype(f32)
    east = flag_east.astype(f32)
    north = flag_north.astype(f32)

    step = divisor(levels, 4)
    modes_level = pl.BlockSpec((count, step, size_x, size_y), lambda z: (0, z, 0, 0))
    layers = pl.BlockSpec((step, HALO * count, size_y), lambda z: (z, 0, 0))
    whole_plane = pl.BlockSpec((levels, size_x, size_y), lambda z: (0, 0, 0))
    side_rows = (HALO + 3, HALO + 1)
    x_last, x_first, aux_last, aux_first = pl.pallas_call(
        layers_kernel,
        grid=(levels // step,),
        in_specs=[modes_level] + [whole_plane] * 4,
        out_specs=[layers, layers] + [pl.BlockSpec((n, levels, size_y), lambda z: (0, 0, 0)) for n in side_rows],
        out_shape=[jax.ShapeDtypeStruct((levels, HALO * count, size_y), f32)] * 2
        + [jax.ShapeDtypeStruct((n, levels, size_y), f32) for n in side_rows],
    )(mode_fields, mean_field, velocity_east, flag_east, ocean_mask)
    aux_before = up(aux_last, "gx")
    aux_after = down(aux_first, "gx")
    x_before = up(x_last, "gx")
    x_after = down(x_first, "gx")
    aux_before = aux_before.transpose(1, 0, 2)
    aux_after = aux_after.transpose(1, 0, 2)

    half = SUB if levels % SUB == 0 else levels
    plane = pl.BlockSpec((half, size_x, size_y), lambda z: (z, 0, 0))
    columns = pl.BlockSpec((half, size_x, LANES), lambda z: (z, 0, 0))
    y_last, y_first = pl.pallas_call(
        columns_kernel,
        grid=(levels // half,),
        in_specs=[pl.BlockSpec(memory_space=pl.ANY)]
        + [pl.BlockSpec((count, half, size_x, size_y), lambda z: (0, z, 0, 0))]
        + [plane] * 4,
        out_specs=[columns, columns],
        out_shape=[jax.ShapeDtypeStruct((levels, size_x, LANES), f32)] * 2,
    )(x_last, mode_fields, mean_field, velocity_north, flag_north, ocean_mask)
    y_before, y_after = up(y_last, "gy"), down(y_first, "gy")

    speed = jnp.concatenate([aux_before[:, 4:5], velocity_east], axis=1)
    side = jnp.concatenate([aux_before[:, 5:6], east], axis=1)
    cells = jnp.concatenate([aux_before[:, 3:4], wet, aux_after[:, 3:4]], axis=1)
    dx = stencil(speed * side, speed * (1.0 - side), cells[:, :-1] * cells[:, 1:], wet, 1)
    at = HALO * count
    speed = jnp.concatenate([y_before[:, :, at + 4 : at + 5], velocity_north], axis=2)
    side = jnp.concatenate([y_before[:, :, at + 5 : at + 6], north], axis=2)
    cells = jnp.concatenate([y_before[:, :, at + 3 : at + 4], wet, y_after[:, :, at + 3 : at + 4]], axis=2)
    dy = stencil(speed * side, speed * (1.0 - side), cells[:, :, :-1] * cells[:, :, 1:], wet, 2)
    centre = dx[0] + dy[0] - 2.0 * vert_diff * wet
    vertical = vert_diff * wet

    shifts = (-3, -2, -1, 1, 2, 3)
    spot = lax.broadcasted_iota(jnp.int32, (levels, size_x, size_y), 1)
    inner = [jnp.where((spot + s >= 0) & (spot + s < size_x), dx[s], 0.0) for s in shifts]
    outer = [
        jnp.where(spot + s < 0, dx[s], 0.0)[:, :SUB] if s < 0 else jnp.where(spot + s >= size_x, dx[s], 0.0)[:, -SUB:]
        for s in shifts
    ]

    mean_x = jnp.concatenate([aux_before[:, :HALO], mean_field, aux_after[:, :HALO]], axis=1)
    mean_y = jnp.concatenate([y_before[:, :, at : at + HALO], mean_field, y_after[:, :, at : at + HALO]], axis=2)
    above = jnp.concatenate([mean_field[1:], mean_field[-1:]], axis=0)
    below = jnp.concatenate([mean_field[:1], mean_field[:-1]], axis=0)
    mean_tend = centre * mean_field + vertical * (above + below)
    for s in shifts:
        mean_tend = mean_tend + dx[s] * lax.slice_in_dim(mean_x, HALO + s, HALO + s + size_x, axis=1)
        mean_tend = mean_tend + dy[s] * lax.slice_in_dim(mean_y, HALO + s, HALO + s + size_y, axis=2)
    mean_next = mean_field + time_step * mean_tend

    group = divisor(count, 2)
    one_field = pl.BlockSpec((group, levels, size_x, size_y), lambda f: (f, 0, 0, 0))
    grid_whole = pl.BlockSpec((levels, size_x, size_y), lambda f: (0, 0, 0))
    halo_whole = pl.BlockSpec((levels, size_x, LANES), lambda f: (0, 0, 0))
    cost = pl.CostEstimate(flops=60 * mode_fields.size, bytes_accessed=12 * mode_fields.size, transcendentals=0)
    partial = pl.pallas_call(
        interior_kernel,
        grid=(count // group,),
        in_specs=[one_field, halo_whole, halo_whole] + [grid_whole] * 14,
        out_specs=one_field,
        out_shape=jax.ShapeDtypeStruct(mode_fields.shape, f32),
        cost_estimate=cost,
    )(mode_fields, y_before, y_after, *inner, *[dy[s] for s in shifts], centre, vertical)

    edge = pl.BlockSpec((step, SUB, size_y), lambda z: (z, 0, 0))
    wide = 2 * count * SUB
    packed = (4 * count * count // LANES, LANES)
    tend, gram = pl.pallas_call(
        functools.partial(gram_kernel, nx, ny),
        grid=(levels // step,),
        in_specs=[modes_level, modes_level, layers, layers] + [edge] * 6,
        out_specs=[modes_level, pl.BlockSpec(packed, lambda z: (0, 0))],
        out_shape=[jax.ShapeDtypeStruct(mode_fields.shape, f32), jax.ShapeDtypeStruct(packed, f32)],
        scratch_shapes=[pltpu.VMEM((step, HALO * count + 2 * SUB, size_y), f32)] * 2
        + [
            pltpu.VMEM((2 * wide, wide), f32),
            pltpu.VMEM(packed, f32),
            pltpu.VMEM((nx * ny,) + packed, f32),
            pltpu.SemaphoreType.DMA((nx * ny,)),
            pltpu.SemaphoreType.DMA((nx * ny,)),
        ],
        compiler_params=pltpu.CompilerParams(collective_id=0, has_side_effects=True),
    )(mode_fields, partial, x_before, x_after, *outer)

    cell_count = float(levels * size_x * size_y * nx * ny)
    modes_next, factor = pl.pallas_call(
        functools.partial(combine_kernel, cell_count),
        grid=(levels // step,),
        in_specs=[pl.BlockSpec(packed, lambda z: (0, 0)), modes_level, modes_level],
        out_specs=[modes_level, pl.BlockSpec((count, count), lambda z: (0, 0))],
        out_shape=[jax.ShapeDtypeStruct(mode_fields.shape, f32), jax.ShapeDtypeStruct((count, count), f32)],
        scratch_shapes=[pltpu.VMEM((wide, wide), jnp.bfloat16)],
    )(gram, mode_fields, tend)
    return (mean_next, modes_next, factor)


def solution(mesh):
    grid = P(None, "gx", "gy")
    return jax.shard_map(
        section,
        mesh=mesh,
        in_specs=(grid, P(None, None, "gx", "gy"), grid, grid, grid, grid, grid),
        out_specs=(grid, P(None, None, "gx", "gy"), P()),
        check_vma=False,
    )
```

profile of v0, /device:TPU:0, one launch (start us, length us, event | category | flops | bytes accessed | tf_op | source)
XLA Modules:
  0.0 84.6 jit_solution(7103389391182863655)
XLA Ops:
  0.6 4.7 %shard_map.94 = (f32[16,48,256]{2,1,0:T(8,128)}, f32[16,48,256]{2,1,0:T(8,128)}, f32[6,16,256]{2,1,0:T(8,128)}, f32[4,16,256]{2,1,0:T(8,128)}) custom-call(f32[16,16,16,256]{3,2,1,0:T(8,128)} %modes.7, f32[16,16,256]{2,1,0:T(8,128)} %mean.3, f32[16,16,256]{2,1,0:T(8,128)} %east.1, s32[16,16,256]{2,1,0:T(8,128)} %flag.1, s32[16,16,256]{2,1,0:T(8,128)} %mask.3), custom_call_target="tpu_custom_call" | custom-call | tf_op jit(solution)/shard_map/pallas_call | solution.py:353
  5.3 1.0 %copy.11 = f32[4,16,256]{2,0,1:T(4,128)S(1)} copy(f32[4,16,256]{2,1,0:T(8,128)} %get-tuple-element.14) | data formatting | bytes 131072 | tf_op jit(solution)/shard_map/pallas_call | solution.py:353
  6.3 1.3 %collective-permute-start.1 = (f32[4,16,256]{2,0,1:T(4,128)S(1)}, f32[4,16,256]{2,0,1:T(4,128)S(1)}, u32[]{:S(2)}, u32[]{:S(2)}) collective-permute-start(f32[4,16,256]{2,0,1:T(4,128)S(1)} %copy.11), channel_id=1, source_target_pairs={{4,0},{8,4},{12,8},{16,12},{20,16},{24,20},{28,24},{5,1},{9,5},{13... | collective-permute-start | bytes 196616 | tf_op jit(solution)/shard_map/ppermute | solution.py:342
  7.6 1.0 %copy.10 = f32[6,16,256]{2,0,1:T(8,128)S(1)} copy(f32[6,16,256]{2,1,0:T(8,128)} %get-tuple-element.13) | data formatting | bytes 196608 | tf_op jit(solution)/shard_map/pallas_call | solution.py:353
  8.6 5.5 %collective-permute-start = (f32[6,16,256]{2,0,1:T(8,128)S(1)}, f32[6,16,256]{2,0,1:T(8,128)S(1)}, u32[]{:S(2)}, u32[]{:S(2)}) collective-permute-start(f32[6,16,256]{2,0,1:T(8,128)S(1)} %copy.10), channel_id=1, source_target_pairs={{0,4},{4,8},{8,12},{12,16},{16,20},{20,24},{24,28},{1,5},{5,9},{9,... | collective-permute-start | bytes 294920 | tf_op jit(solution)/shard_map/ppermute | solution.py:339
  14.1 5.0 %collective-permute-start.4 = (f32[16,48,256]{2,1,0:T(8,128)}, f32[16,48,256]{2,1,0:T(8,128)S(1)}, u32[]{:S(2)}, u32[]{:S(2)}) collective-permute-start(f32[16,48,256]{2,1,0:T(8,128)} %get-tuple-element.15.after_layers), channel_id=1, source_target_pairs={{0,4},{4,8},{8,12},{12,16},{16,20},{20,24},{24,28},{1,5},{5,9},{9,... | collective-permute-start | bytes 2359304 | tf_op jit(solution)/shard_map/ppermute | solution.py:339
  19.1 3.8 %shard_map.95 = (f32[16,16,128]{2,1,0:T(8,128)}, f32[16,16,128]{2,1,0:T(8,128)}) custom-call(f32[16,48,256]{2,1,0:T(8,128)} %get-tuple-element.15.after_layers, f32[16,16,16,256]{3,2,1,0:T(8,128)} %modes.7, f32[16,16,256]{2,1,0:T(8,128)} %mean.3, f32[16,16,256]{2,1,0:T(8,128)} %north.1, s32[16,16,256]{2,1,0:T(8,128)} %flag_north.1, s32[16,16,256]{2,1,0:T(8,128)} %mask.3), custom_call_target="tpu_custom_call" | custom-call | tf_op jit(solution)/shard_map/pallas_call | solution.py:371
  22.9 1.3 %collective-permute-start.2 = (f32[16,16,128]{2,1,0:T(8,128)}, f32[16,16,128]{2,1,0:T(8,128)S(1)}, u32[]{:S(2)}, u32[]{:S(2)}) collective-permute-start(f32[16,16,128]{2,1,0:T(8,128)} %get-tuple-element.16), channel_id=1, source_target_pairs={{0,1},{1,2},{2,3},{4,5},{5,6},{6,7},{8,9},{9,10},{10,11},{12,13},{... | collective-permute-start | bytes 393224 | tf_op jit(solution)/shard_map/ppermute | solution.py:339
  24.2 1.3 %collective-permute-start.3 = (f32[16,16,128]{2,1,0:T(8,128)}, f32[16,16,128]{2,1,0:T(8,128)S(1)}, u32[]{:S(2)}, u32[]{:S(2)}) collective-permute-start(f32[16,16,128]{2,1,0:T(8,128)} %get-tuple-element.17), channel_id=1, source_target_pairs={{1,0},{2,1},{3,2},{5,4},{6,5},{7,6},{9,8},{10,9},{11,10},{13,12},{... | collective-permute-start | bytes 393224 | tf_op jit(solution)/shard_map/ppermute | solution.py:342
  25.8 0.1 slice.310
  25.9 0.1 slice.312
  26.1 1.3 %collective-permute-start.5 = (f32[16,48,256]{2,1,0:T(8,128)S(1)}, f32[16,48,256]{2,1,0:T(8,128)S(1)}, u32[]{:S(2)}, u32[]{:S(2)}) collective-permute-start(f32[16,48,256]{2,1,0:T(8,128)S(1)} %copy-done.10), channel_id=1, source_target_pairs={{4,0},{8,4},{12,8},{16,12},{20,16},{24,20},{28,24},{5,1},{9,5},{13... | collective-permute-start | bytes 2359304 | tf_op jit(solution)/shard_map/ppermute | solution.py:342
  27.5 0.3 add_multiply_fusion.2
  27.8 0.3 multiply_multiply_fusion.5
  28.1 0.3 add_multiply_fusion.3
  28.4 1.5 %broadcast_select_fusion.3 = (f32[16,16,256]{2,1,0:T(8,128)}, f32[16,16,256]{2,1,0:T(8,128)S(1)}, f32[16,16,256]{2,1,0:T(8,128)}, f32[16,16,256]{2,1,0:T(8,128)S...) fusion(pred[16]{0:T(512)(128)(4,1)S(1)} %compare_and_fusion.3, ...), kind=kLoop, calls=%fused_computation.115 | loop fusion | flops 1245184 | bytes 6291552 | tf_op jit(solution)/shard_map/jit(_where)/select_n | solution.py:396
  29.9 0.8 slice_select_fusion.2
  30.7 0.8 slice_select_fusion.4
  31.5 0.8 slice_select_fusion
  32.3 0.1 slice.259
  32.4 0.2 fusion.71
  32.6 0.4 add_multiply_fusion
  33.0 0.2 multiply_multiply_fusion
  33.2 0.1 slice.269
  33.3 0.1 slice.291
  33.4 0.3 multiply_multiply_fusion.2
  33.7 2.3 %fusion.8 = (f32[16,16,256]{2,1,0:T(8,128)}, f32[16,16,256]{2,1,0:T(8,128)}, f32[16,16,256]{2,1,0:T(8,128)}, f32[16,16,256]{2,1,0:T(8,128)}, f32[16,16,256]{2,1,...) fusion(f32[16,16,256]{2,1,0:T(8,128)S(1)} %copy-done.1, ...), kind=kLoop, calls=%fused_computation.44 | loop fusion | flops 4128768 | bytes 8493056 | tf_op jit(solution)/shard_map/add | solution.py:410
  36.0 17.7 %shard_map.96.partial = f32[16,16,16,256]{3,2,1,0:T(8,128)} custom-call(f32[16,16,16,256]{3,2,1,0:T(8,128)} %modes.7, f32[16,16,128]{2,1,0:T(8,128)} %copy-done.3, f32[16,16,128]{2,1,0:T(8,128)} %copy-done.4, f32[16,16,256]{2,1,0:T(8,128)} %get-tuple-element.58.rest_0_, f32[16,16,256]{2,1,0:T(8,128)} %get-tuple-element.56.rest_1_, ...), custom_call_target="tpu_custom_call" | custom-call | flops 62914560 | bytes 12582912 | tf_op jit(solution)/shard_map/pallas_call | solution.py:417
  53.7 0.9 %copy-done.9 = f32[16,48,256]{2,1,0:T(8,128)} copy-done((f32[16,48,256]{2,1,0:T(8,128)}, f32[16,48,256]{2,1,0:T(8,128)S(1)}, u32[]{:S(2)}) %copy-start.9) | copy-done | bytes 786456
  54.6 0.3 copy-done.8
  54.8 20.6 %shard_map.97 = (f32[16,16,16,256]{3,2,1,0:T(8,128)}, f32[8,128]{1,0:T(8,128)}) custom-call(f32[16,16,16,256]{3,2,1,0:T(8,128)} %modes.7, f32[16,16,16,256]{3,2,1,0:T(8,128)} %shard_map.96.partial, f32[16,48,256]{2,1,0:T(8,128)} %copy-done.8, f32[16,48,256]{2,1,0:T(8,128)} %copy-done.9, f32[16,8,256]{2,1,0:T(8,128)} %get-tuple-element.86.l3, ...), custom_call_target="tpu_custom_call" | custom-call | tf_op jit(solution)/shard_map/pallas_call | solution.py:429
  75.4 9.2 %shard_map.98 = (f32[16,16,16,256]{3,2,1,0:T(8,128)}, f32[16,16]{1,0:T(8,128)}) custom-call(f32[8,128]{1,0:T(8,128)} %get-tuple-element.19.packed, f32[16,16,16,256]{3,2,1,0:T(8,128)} %modes.7, f32[16,16,16,256]{3,2,1,0:T(8,128)} %get-tuple-element.20.tend), custom_call_target="tpu_custom_call" | custom-call | tf_op jit(solution)/shard_map/pallas_call | solution.py:447
  (47 shorter events, 0.4 us)
Async XLA Ops:
  5.3 20.4 %copy-start.1 = (f32[16,16,256]{2,1,0:T(8,128)S(1)}, f32[16,16,256]{2,1,0:T(8,128)}, u32[]{:S(2)}) copy-start(f32[16,16,256]{2,1,0:T(8,128)} %mean.3) | copy-start | bytes 786436
  5.3 20.4 %copy-start = (s32[16,16,256]{2,1,0:T(8,128)S(1)}, s32[16,16,256]{2,1,0:T(8,128)}, u32[]{:S(2)}) copy-start(s32[16,16,256]{2,1,0:T(8,128)} %mask.3) | copy-start | bytes 786436
  5.3 20.4 %copy-start.6 = (s32[16,16,256]{2,1,0:T(8,128)S(1)}, s32[16,16,256]{2,1,0:T(8,128)}, u32[]{:S(2)}) copy-start(s32[16,16,256]{2,1,0:T(8,128)} %flag.1) | copy-start | bytes 786436
  5.3 20.4 %copy-start.7 = (s32[16,16,256]{2,1,0:T(8,128)S(1)}, s32[16,16,256]{2,1,0:T(8,128)}, u32[]{:S(2)}) copy-start(s32[16,16,256]{2,1,0:T(8,128)} %flag_north.1) | copy-start | bytes 786436
  6.3 19.8 %collective-permute-start.1 = (f32[4,16,256]{2,0,1:T(4,128)S(1)}, f32[4,16,256]{2,0,1:T(4,128)S(1)}, u32[]{:S(2)}, u32[]{:S(2)}) collective-permute-start(f32[4,16,256]{2,0,1:T(4,128)S(1)} %copy.11), channel_id=1, source_target_pairs={{4,0},{8,4},{12,8},{16,12},{20,16},{24,20},{28,24},{5,1},{9,5},{13... | collective-permute-start | bytes 196616 | tf_op jit(solution)/shard_map/ppermute | solution.py:342
  8.6 18.9 %collective-permute-start = (f32[6,16,256]{2,0,1:T(8,128)S(1)}, f32[6,16,256]{2,0,1:T(8,128)S(1)}, u32[]{:S(2)}, u32[]{:S(2)}) collective-permute-start(f32[6,16,256]{2,0,1:T(8,128)S(1)} %copy.10), channel_id=1, source_target_pairs={{0,4},{4,8},{8,12},{12,16},{16,20},{20,24},{24,28},{1,5},{5,9},{9,... | collective-permute-start | bytes 294920 | tf_op jit(solution)/shard_map/ppermute | solution.py:339
  14.1 12.0 %copy-start.10 = (f32[16,48,256]{2,1,0:T(8,128)S(1)}, f32[16,48,256]{2,1,0:T(8,128)}, u32[]{:S(2)}) copy-start(f32[16,48,256]{2,1,0:T(8,128)} %get-tuple-element.18) | copy-start | bytes 2359300
  14.1 13.4 %copy-start.2 = (f32[16,16,256]{2,1,0:T(8,128)S(1)}, f32[16,16,256]{2,1,0:T(8,128)}, u32[]{:S(2)}) copy-start(f32[16,16,256]{2,1,0:T(8,128)} %east.1) | copy-start | bytes 786436
  14.1 39.6 %collective-permute-start.4 = (f32[16,48,256]{2,1,0:T(8,128)}, f32[16,48,256]{2,1,0:T(8,128)S(1)}, u32[]{:S(2)}, u32[]{:S(2)}) collective-permute-start(f32[16,48,256]{2,1,0:T(8,128)} %get-tuple-element.15.after_layers), channel_id=1, source_target_pairs={{0,4},{4,8},{8,12},{12,16},{16,20},{20,24},{24,28},{1,5},{5,9},{9,... | collective-permute-start | bytes 2359304 | tf_op jit(solution)/shard_map/ppermute | solution.py:339
  22.9 9.5 %collective-permute-start.2 = (f32[16,16,128]{2,1,0:T(8,128)}, f32[16,16,128]{2,1,0:T(8,128)S(1)}, u32[]{:S(2)}, u32[]{:S(2)}) collective-permute-start(f32[16,16,128]{2,1,0:T(8,128)} %get-tuple-element.16), channel_id=1, source_target_pairs={{0,1},{1,2},{2,3},{4,5},{5,6},{6,7},{8,9},{9,10},{10,11},{12,13},{... | collective-permute-start | bytes 393224 | tf_op jit(solution)/shard_map/ppermute | solution.py:339
  24.2 8.1 %collective-permute-start.3 = (f32[16,16,128]{2,1,0:T(8,128)}, f32[16,16,128]{2,1,0:T(8,128)S(1)}, u32[]{:S(2)}, u32[]{:S(2)}) collective-permute-start(f32[16,16,128]{2,1,0:T(8,128)} %get-tuple-element.17), channel_id=1, source_target_pairs={{1,0},{2,1},{3,2},{5,4},{6,5},{7,6},{9,8},{10,9},{11,10},{13,12},{... | collective-permute-start | bytes 393224 | tf_op jit(solution)/shard_map/ppermute | solution.py:342
  26.1 27.6 %collective-permute-start.5 = (f32[16,48,256]{2,1,0:T(8,128)S(1)}, f32[16,48,256]{2,1,0:T(8,128)S(1)}, u32[]{:S(2)}, u32[]{:S(2)}) collective-permute-start(f32[16,48,256]{2,1,0:T(8,128)S(1)} %copy-done.10), channel_id=1, source_target_pairs={{4,0},{8,4},{12,8},{16,12},{20,16},{24,20},{28,24},{5,1},{9,5},{13... | collective-permute-start | bytes 2359304 | tf_op jit(solution)/shard_map/ppermute | solution.py:342
  28.4 4.2 %copy-start.5 = (f32[16,16,256]{2,1,0:T(8,128)S(1)}, f32[16,16,256]{2,1,0:T(8,128)}, u32[]{:S(2)}) copy-start(f32[16,16,256]{2,1,0:T(8,128)} %north.1) | copy-start | bytes 786436
  32.3 3.7 %copy-start.4 = (f32[16,16,128]{2,1,0:T(8,128)}, f32[16,16,128]{2,1,0:T(8,128)S(1)}, u32[]{:S(2)}) copy-start(f32[16,16,128]{2,1,0:T(8,128)S(1)} %collective-permute-done.3.after) | copy-start | bytes 393220
  32.4 3.6 %copy-start.3 = (f32[16,16,128]{2,1,0:T(8,128)}, f32[16,16,128]{2,1,0:T(8,128)S(1)}, u32[]{:S(2)}) copy-start(f32[16,16,128]{2,1,0:T(8,128)S(1)} %collective-permute-done.2.before) | copy-start | bytes 393220
  53.7 0.9 %copy-start.9 = (f32[16,48,256]{2,1,0:T(8,128)}, f32[16,48,256]{2,1,0:T(8,128)S(1)}, u32[]{:S(2)}) copy-start(f32[16,48,256]{2,1,0:T(8,128)S(1)} %collective-permute-done.5.high) | copy-start | bytes 2359300
  53.7 1.1 %copy-start.8 = (f32[16,48,256]{2,1,0:T(8,128)}, f32[16,48,256]{2,1,0:T(8,128)S(1)}, u32[]{:S(2)}) copy-start(f32[16,48,256]{2,1,0:T(8,128)S(1)} %collective-permute-done.4.low) | copy-start | bytes 2359300
where the time goes:
time: 85.1 us; the launch traced here: 84.6 us
  Pallas kernels  55.9 us (66%)
  starting transfers between devices  15.7 us (18%)
  other arithmetic  8.1 us (10%)
  local copies, waits for them, and re-layouts  3.89 us (5%)
  between operations  1.04 us (1%)
    pallas_call x1, Pallas kernels, section(): pl.pallas_call(functools.partial(gram_kernel, nx, ny), grid=(levels // st...  20.6 us
    pallas_call x1, Pallas kernels, section(): pl.pallas_call(interior_kernel, grid=(count // group,), in_specs=[one_fie...  17.7 us
    ppermute x3, starting transfers between devices, up(): lax.ppermute(value, axis, [(i, i + 1) for i in range(lax.axis_size(axis)...  11.8 us
    pallas_call x1, Pallas kernels, section(): pl.pallas_call(functools.partial(combine_kernel, cell_count), grid=(level...  9.2 us
    pallas_call x1, Pallas kernels, section(): pl.pallas_call(layers_kernel, grid=(levels // step,), in_specs=[modes_lev...  4.67 us
    ppermute x3, starting transfers between devices, down(): lax.ppermute(value, axis, [(i + 1, i) for i in range(lax.axis_size(axis)...  3.88 us
    pallas_call x1, Pallas kernels, section(): pl.pallas_call(columns_kernel, grid=(levels // half,), in_specs=[pl.Block...  3.81 us
    add x1, other arithmetic, section(): mean_next = mean_field + time_step * mean_tend  2.3 us
  transfers between devices with their start and end apart: 6, of which 0 were waited for; matrix products, arithmetic and copies ran while one was open for 12% of the time, Pallas kernels for 25%

commit v1 on v0

--- a/solution.py
+++ b/solution.py
@@ -64,33 +64,127 @@
         y_first[k] = first
 
 
-def interior_kernel(field, before, after, *rest):
-    coefs_x, coefs_y, centre, vertical, out = rest[:6], rest[6:12], rest[12], rest[13], rest[14]
+def face_weights(pos, neg, openness):
+    return {
+        -2: openness * (2.0 * pos) / 60.0,
+        -1: openness * (-13.0 * pos - 3.0 * neg) / 60.0,
+        0: openness * ((47.0 * pos + 27.0 * neg) / 60.0 + horiz_diff),
+        1: openness * ((27.0 * pos + 47.0 * neg) / 60.0 - horiz_diff),
+        2: openness * (-3.0 * pos - 13.0 * neg) / 60.0,
+        3: openness * (2.0 * neg) / 60.0,
+    }
+
+
+def stencil(speed, side, cells, speed_before, side_before, cells_before, cells_after, axis):
+    size = cells.shape[axis]
+    spot = lax.broadcasted_iota(jnp.int32, cells.shape, axis)
+    beyond = jnp.where(spot == size - 1, cells_after, pltpu.roll(cells, size - 1, axis))
+    face = face_weights(speed * side, speed * (1.0 - side), cells * beyond)
+    first = cells[:1, :] if axis == 0 else cells[:, :1]
+    entry = face_weights(speed_before * side_before, speed_before * (1.0 - side_before), cells_before * first)
+    result = {}
+    for s in range(-3, 4):
+        value = 0.0
+        if s + 1 in face:
+            value = value + jnp.where(spot == 0, entry[s + 1], pltpu.roll(face[s + 1], 1, axis))
+        if s in face:
+            value = value - face[s]
+        result[s] = cells * value
+    return result
+
+
+def interior_kernel(
+    field, mean, east, north, flag_east, flag_north, mask, side_before, side_after, before, after,
+    out, mean_next, l3, l2, l1, h1, h2, h3, *coefs,
+):
+    coefs_x, coefs_y, centre, vertical = coefs[:6], coefs[6:12], coefs[12], coefs[13]
     group, levels, size_x, size_y = field.shape
+    modes = group * pl.num_programs(0)
     f0 = pl.program_id(0) * group
     lane = lax.broadcasted_iota(jnp.int32, (size_x, LANES), 1)
     tiles = size_y // LANES
     shifts = (-3, -2, -1, 1, 2, 3)
 
+    def columns_around(k, f, read):
+        left = pltpu.roll(before[k], LANES - HALO - HALO * f, 1)
+        right = pltpu.roll(after[k], LANES - HALO * f, 1)
+        return [left] + [read(slice(t * LANES, (t + 1) * LANES)) for t in range(tiles)] + [right]
+
+    def moved(row, t, s):
+        if s < 0:
+            mixed = jnp.where(lane >= LANES + s, row[t], row[t + 1])
+        else:
+            mixed = jnp.where(lane < s, row[t + 2], row[t + 1])
+        return pltpu.roll(mixed, (-s) % LANES, 1)
+
+    @pl.when(pl.program_id(0) == 0)
+    def _():
+        spot = lax.broadcasted_iota(jnp.int32, (size_x, size_y), 0)
+        at = HALO * field.shape[0] * pl.num_programs(0)
+        column = lax.broadcasted_iota(jnp.int32, (size_x, LANES), 1)
+
+        def picked(ref, k, offset):
+            return jnp.sum(jnp.where(column == at + offset, ref[k], 0.0), axis=1, keepdims=True)
+
+        def prepare(k, carry):
+            wet = mask[k].astype(jnp.float32)
+            low = [side_before[j, pl.ds(k, 1), :] for j in range(HALO + 3)]
+            high = [side_after[j, pl.ds(k, 1), :] for j in range(HALO + 1)]
+            dx = stencil(
+                east[k], flag_east[k].astype(jnp.float32), wet, low[HALO + 1], low[HALO + 2], low[HALO], high[HALO], 0
+            )
+            dy = stencil(
+                north[k],
+                flag_north[k].astype(jnp.float32),
+                wet,
+                picked(before, k, HALO + 1),
+                picked(before, k, HALO + 2),
+                picked(before, k, HALO),
+                picked(after, k, HALO),
+                1,
+            )
+            middle = dx[0] + dy[0] - 2.0 * vert_diff * wet
+            upright = vert_diff * wet
+            centre[k] = middle
+            vertical[k] = upright
+            c = mean[k]
+            around = mean[jnp.minimum(k + 1, levels - 1)] + mean[jnp.maximum(k - 1, 0)]
+            total = middle * c + upright * around
+            row = columns_around(k, modes, lambda cut: mean[k, :, cut])
+            for i, s in enumerate(shifts):
+                inside = (spot + s >= 0) & (spot + s < size_x)
+                coefs_x[i][k] = jnp.where(inside, dx[s], 0.0)
+                outside = jnp.where(inside, 0.0, dx[s])
+                if s < 0:
+                    (l3, l2, l1)[i][k] = outside[:SUB]
+                else:
+                    (h1, h2, h3)[i - 3][k] = outside[size_x - SUB :]
+                coefs_y[i][k] = dy[s]
+                shifted = pltpu.roll(c, (-s) % size_x, 0)
+                for j in range(abs(s)):
+                    if s < 0:
+                        shifted = jnp.where(spot == j, low[HALO + s + j], shifted)
+                    else:
+                        shifted = jnp.where(spot == size_x - s + j, high[j], shifted)
+                total += dx[s] * shifted
+                total += dy[s] * jnp.concatenate([moved(row, t, s) for t in range(tiles)], axis=1)
+            mean_next[k] = c + time_step * total
+            return carry
+
+        lax.fori_loop(0, levels, prepare, 0)
+
     def level(k, carry):
         above = jnp.minimum(k + 1, levels - 1)
         below = jnp.maximum(k - 1, 0)
         for g in range(group):
-            f = f0 + g
-            left = pltpu.roll(before[k], LANES - HALO - HALO * f, 1)
-            right = pltpu.roll(after[k], LANES - HALO * f, 1)
-            row = [left] + [field[g, k, :, t * LANES : (t + 1) * LANES] for t in range(tiles)] + [right]
+            row = columns_around(k, f0 + g, lambda cut: field[g, k, :, cut])
             for t in range(tiles):
                 cut = slice(t * LANES, (t + 1) * LANES)
                 c = row[t + 1]
                 total = centre[k, :, cut] * c + vertical[k, :, cut] * (field[g, above, :, cut] + field[g, below, :, cut])
                 for i, s in enumerate(shifts):
                     total += coefs_x[i][k, :, cut] * pltpu.roll(c, (-s) % size_x, 0)
-                    if s < 0:
-                        mixed = jnp.where(lane >= LANES + s, row[t], c)
-                    else:
-                        mixed = jnp.where(lane < s, row[t + 2], c)
-                    total += coefs_y[i][k, :, cut] * pltpu.roll(mixed, (-s) % LANES, 1)
+                    total += coefs_y[i][k, :, cut] * moved(row, t, s)
                 out[g, k, :, cut] = total
         return carry
 
@@ -99,38 +193,48 @@
 
 def gram_kernel(
     nx, ny, modes, partial, low, high, l3, l2, l1, h1, h2, h3, tend, gram,
-    low_rows, high_rows, total, mine, gathered, send_sem, recv_sem,
+    low_rows, high_rows, total, mine, middle, along_y, along_x, send_y, recv_y, send_x, recv_x,
 ):
     z = pl.program_id(0)
-    me = lax.axis_index("gx") * ny + lax.axis_index("gy")
-    devices = nx * ny
+    gx, gy = lax.axis_index("gx"), lax.axis_index("gy")
     barrier = pltpu.get_barrier_semaphore()
     count, levels, size_x, size_y = modes.shape
 
-    def place(k):
-        other = lax.rem(me + k, devices)
-        return other, (other // ny, lax.rem(other, ny))
-
-    def copy(k, slot):
+    rows = low.shape[1]
+    wide = 2 * count * SUB
+
+    def next_y(k):
+        return lax.rem(gy + k, ny)
+
+    def next_x(k):
+        return lax.rem(gx + k, nx)
+
+    def copy_y(k, slot):
         return pltpu.make_async_remote_copy(
             src_ref=mine,
-            dst_ref=gathered.at[slot],
-            send_sem=send_sem.at[k],
-            recv_sem=recv_sem.at[slot],
-            device_id=place(k)[1],
+            dst_ref=along_y.at[slot],
+            send_sem=send_y.at[k],
+            recv_sem=recv_y.at[slot],
+            device_id=(gx, next_y(k)),
             device_id_type=MESH,
         )
 
-    rows = low.shape[1]
-    wide = 2 * count * SUB
+    def copy_x(k, slot):
+        return pltpu.make_async_remote_copy(
+            src_ref=middle,
+            dst_ref=along_x.at[slot],
+            send_sem=send_x.at[k],
+            recv_sem=recv_x.at[slot],
+            device_id=(next_x(k), gy),
+            device_id_type=MESH,
+        )
 
     @pl.when(z == 0)
     def _():
-        def greet(k, carry):
-            pl.semaphore_signal(barrier, inc=1, device_id=place(k)[1], device_id_type=MESH)
-            return carry
-
-        lax.fori_loop(1, devices, greet, 0)
+        for k in range(1, ny):
+            pl.semaphore_signal(barrier, inc=1, device_id=(gx, next_y(k)), device_id_type=MESH)
+        for k in range(1, nx):
+            pl.semaphore_signal(barrier, inc=1, device_id=(next_x(k), gy), device_id_type=MESH)
         low_rows[...] = jnp.zeros_like(low_rows)
         high_rows[...] = jnp.zeros_like(high_rows)
         total[...] = jnp.zeros_like(total)
@@ -193,28 +297,29 @@
         for b in range(1, 2 * count // height):
             packed = jnp.where(block == b, full[b * height : (b + 1) * height], packed)
         mine[...] = packed
-        gathered[me] = packed
-        pl.semaphore_wait(barrier, devices - 1)
-
-        def send(k, carry):
-            copy(k, me).start()
-            return carry
-
-        def arrive(k, carry):
-            copy(k, place(k)[0]).wait_recv()
-            return carry
-
-        def sent(k, carry):
-            copy(k, me).wait_send()
-            return carry
-
-        def add(k, value):
-            return value + gathered[k]
-
-        lax.fori_loop(1, devices, send, 0)
-        lax.fori_loop(1, devices, arrive, 0)
-        gram[...] = lax.fori_loop(1, devices, add, gathered[0])
-        lax.fori_loop(1, devices, sent, 0)
+        along_y[gy] = packed
+        pl.semaphore_wait(barrier, nx + ny - 2)
+        for k in range(1, ny):
+            copy_y(k, gy).start()
+        for k in range(1, ny):
+            copy_y(k, next_y(k)).wait_recv()
+        summed = along_y[0]
+        for k in range(1, ny):
+            summed = summed + along_y[k]
+        middle[...] = summed
+        along_x[gx] = summed
+        for k in range(1, ny):
+            copy_y(k, gy).wait_send()
+        for k in range(1, nx):
+            copy_x(k, gx).start()
+        for k in range(1, nx):
+            copy_x(k, next_x(k)).wait_recv()
+        summed = along_x[0]
+        for k in range(1, nx):
+            summed = summed + along_x[k]
+        gram[...] = summed
+        for k in range(1, nx):
+            copy_x(k, gx).wait_send()
 
 
 def solve(packed, count, cells):
@@ -309,27 +414,6 @@
     return max(d for d in range(1, most + 1) if size % d == 0)
 
 
-def stencil(pos, neg, openness, cells, axis):
-    face = {
-        -2: openness * (2.0 * pos) / 60.0,
-        -1: openness * (-13.0 * pos - 3.0 * neg) / 60.0,
-        0: openness * ((47.0 * pos + 27.0 * neg) / 60.0 + horiz_diff),
-        1: openness * ((27.0 * pos + 47.0 * neg) / 60.0 - horiz_diff),
-        2: openness * (-3.0 * pos - 13.0 * neg) / 60.0,
-        3: openness * (2.0 * neg) / 60.0,
-    }
-    size = cells.shape[axis]
-    result = {}
-    for s in range(-3, 4):
-        value = 0.0
-        if s + 1 in face:
-            value = value + lax.slice_in_dim(face[s + 1], 0, size, axis=axis)
-        if s in face:
-            value = value - lax.slice_in_dim(face[s], 1, size + 1, axis=axis)
-        result[s] = cells * value
-    return result
-
-
 def section(mean_field, mode_fields, velocity_east, velocity_north, flag_east, flag_north, ocean_mask):
     count, levels, size_x, size_y = mode_fields.shape
     nx, ny = lax.axis_size("gx"), lax.axis_size("gy")
@@ -340,10 +424,6 @@
 
     def down(value, axis):
         return lax.ppermute(value, axis, [(i + 1, i) for i in range(lax.axis_size(axis) - 1)])
-
-    wet = ocean_mask.astype(f32)
-    east = flag_east.astype(f32)
-    north = flag_north.astype(f32)
 
     step = divisor(levels, 4)
     modes_level = pl.BlockSpec((count, step, size_x, size_y), lambda z: (0, z, 0, 0))
@@ -362,8 +442,6 @@
     aux_after = down(aux_first, "gx")
     x_before = up(x_last, "gx")
     x_after = down(x_first, "gx")
-    aux_before = aux_before.transpose(1, 0, 2)
-    aux_after = aux_after.transpose(1, 0, 2)
 
     half = SUB if levels % SUB == 0 else levels
     plane = pl.BlockSpec((half, size_x, size_y), lambda z: (z, 0, 0))
@@ -379,49 +457,27 @@
     )(x_last, mode_fields, mean_field, velocity_north, flag_north, ocean_mask)
     y_before, y_after = up(y_last, "gy"), down(y_first, "gy")
 
-    speed = jnp.concatenate([aux_before[:, 4:5], velocity_east], axis=1)
-    side = jnp.concatenate([aux_before[:, 5:6], east], axis=1)
-    cells = jnp.concatenate([aux_before[:, 3:4], wet, aux_after[:, 3:4]], axis=1)
-    dx = stencil(speed * side, speed * (1.0 - side), cells[:, :-1] * cells[:, 1:], wet, 1)
-    at = HALO * count
-    speed = jnp.concatenate([y_before[:, :, at + 4 : at + 5], velocity_north], axis=2)
-    side = jnp.concatenate([y_before[:, :, at + 5 : at + 6], north], axis=2)
-    cells = jnp.concatenate([y_before[:, :, at + 3 : at + 4], wet, y_after[:, :, at + 3 : at + 4]], axis=2)
-    dy = stencil(speed * side, speed * (1.0 - side), cells[:, :, :-1] * cells[:, :, 1:], wet, 2)
-    centre = dx[0] + dy[0] - 2.0 * vert_diff * wet
-    vertical = vert_diff * wet
-
-    shifts = (-3, -2, -1, 1, 2, 3)
-    spot = lax.broadcasted_iota(jnp.int32, (levels, size_x, size_y), 1)
-    inner = [jnp.where((spot + s >= 0) & (spot + s < size_x), dx[s], 0.0) for s in shifts]
-    outer = [
-        jnp.where(spot + s < 0, dx[s], 0.0)[:, :SUB] if s < 0 else jnp.where(spot + s >= size_x, dx[s], 0.0)[:, -SUB:]
-        for s in shifts
-    ]
-
-    mean_x = jnp.concatenate([aux_before[:, :HALO], mean_field, aux_after[:, :HALO]], axis=1)
-    mean_y = jnp.concatenate([y_before[:, :, at : at + HALO], mean_field, y_after[:, :, at : at + HALO]], axis=2)
-    above = jnp.concatenate([mean_field[1:], mean_field[-1:]], axis=0)
-    below = jnp.concatenate([mean_field[:1], mean_field[:-1]], axis=0)
-    mean_tend = centre * mean_field + vertical * (above + below)
-    for s in shifts:
-        mean_tend = mean_tend + dx[s] * lax.slice_in_dim(mean_x, HALO + s, HALO + s + size_x, axis=1)
-        mean_tend = mean_tend + dy[s] * lax.slice_in_dim(mean_y, HALO + s, HALO + s + size_y, axis=2)
-    mean_next = mean_field + time_step * mean_tend
-
     group = divisor(count, 2)
     one_field = pl.BlockSpec((group, levels, size_x, size_y), lambda f: (f, 0, 0, 0))
-    grid_whole = pl.BlockSpec((levels, size_x, size_y), lambda f: (0, 0, 0))
+    plane_whole = pl.BlockSpec((levels, size_x, size_y), lambda f: (0, 0, 0))
     halo_whole = pl.BlockSpec((levels, size_x, LANES), lambda f: (0, 0, 0))
     cost = pl.CostEstimate(flops=60 * mode_fields.size, bytes_accessed=12 * mode_fields.size, transcendentals=0)
-    partial = pl.pallas_call(
+    partial, mean_next, *outer = pl.pallas_call(
         interior_kernel,
         grid=(count // group,),
-        in_specs=[one_field, halo_whole, halo_whole] + [grid_whole] * 14,
-        out_specs=one_field,
-        out_shape=jax.ShapeDtypeStruct(mode_fields.shape, f32),
+        in_specs=[one_field]
+        + [plane_whole] * 6
+        + [pl.BlockSpec((n, levels, size_y), lambda f: (0, 0, 0)) for n in side_rows]
+        + [halo_whole] * 2,
+        out_specs=[one_field, plane_whole] + [pl.BlockSpec((levels, SUB, size_y), lambda f: (0, 0, 0))] * 6,
+        out_shape=[jax.ShapeDtypeStruct(mode_fields.shape, f32), jax.ShapeDtypeStruct(mean_field.shape, f32)]
+        + [jax.ShapeDtypeStruct((levels, SUB, size_y), f32)] * 6,
+        scratch_shapes=[pltpu.VMEM((levels, size_x, size_y), f32)] * 14,
         cost_estimate=cost,
-    )(mode_fields, y_before, y_after, *inner, *[dy[s] for s in shifts], centre, vertical)
+    )(
+        mode_fields, mean_field, velocity_east, velocity_north, flag_east, flag_north, ocean_mask,
+        aux_before, aux_after, y_before, y_after,
+    )
 
     edge = pl.BlockSpec((step, SUB, size_y), lambda z: (z, 0, 0))
     wide = 2 * count * SUB
@@ -436,9 +492,13 @@
         + [
             pltpu.VMEM((2 * wide, wide), f32),
             pltpu.VMEM(packed, f32),
-            pltpu.VMEM((nx * ny,) + packed, f32),
-            pltpu.SemaphoreType.DMA((nx * ny,)),
-            pltpu.SemaphoreType.DMA((nx * ny,)),
+            pltpu.VMEM(packed, f32),
+            pltpu.VMEM((ny,) + packed, f32),
+            pltpu.VMEM((nx,) + packed, f32),
+            pltpu.SemaphoreType.DMA((ny,)),
+            pltpu.SemaphoreType.DMA((ny,)),
+            pltpu.SemaphoreType.DMA((nx,)),
+            pltpu.SemaphoreType.DMA((nx,)),
         ],
         compiler_params=pltpu.CompilerParams(collective_id=0, has_side_effects=True),
     )(mode_fields, partial, x_before, x_after, *outer)

time: 85.1 us -> 105 us (1.23)
  waiting for transfers between devices: 0.02 us -> 23.8 us
  other arithmetic: 8.1 us -> 0 us
  Pallas kernels: 55.9 us -> 61.5 us
  local copies, waits for them, and re-layouts: 3.89 us -> 2.47 us
    ppermute x3, waiting for transfers between devices: 0.01 us -> 14.5 us  [up(): lax.ppermute(value, axis, [(i, i + 1) for i in range(lax.axis_size(axis)...]
    ppermute x3, waiting for transfers between devices: 0.01 us -> 9.3 us  [down(): lax.ppermute(value, axis, [(i + 1, i) for i in range(lax.axis_size(axis)...]
    select_n x4 -> x0, other arithmetic: 3.89 us -> none  [the longest x2 1.6 us: section(): jnp.where(spot + s >= size_x, dx[s], 0.0)[:, -SUB:]]
    pallas_call x1, Pallas kernels: 17.7 us -> 21 us  [section(): pl.pallas_call(interior_kernel, grid=(count // group,), in_specs=[one_fie...]
    add x1 -> x0, other arithmetic: 2.3 us -> none  [section(): mean_next = mean_field + time_step * mean_tend]
    pallas_call x1, Pallas kernels: 20.6 us -> 22.8 us  [section(): pl.pallas_call(functools.partial(gram_kernel, nx, ny), grid=(levels // st...]
    pallas_call x2 -> x0, local copies, waits for them, and re-layouts: 1.93 us -> none  [section(): pl.pallas_call(layers_kernel, grid=(levels // step,), in_specs=[modes_lev...]
    unnamed x22 -> x14, local copies, waits for them, and re-layouts: 1.18 us -> 2.47 us
  transfers between devices with their start and end apart: 6 -> 6, of which waited for: 0 -> 2; matrix products, arithmetic and copies ran while one was open for 12% -> 0% of each run, Pallas kernels for 25% -> 24%
where the time goes in v1:
time: 105 us; the launch traced here: 104 us
  Pallas kernels  61.5 us (59%)
  waiting for transfers between devices  23.8 us (23%)
  starting transfers between devices  15.6 us (15%)
  local copies, waits for them, and re-layouts  2.47 us (2%)
    pallas_call x1, Pallas kernels, section(): pl.pallas_call(functools.partial(gram_kernel, nx, ny), grid=(levels // st...  22.8 us
    pallas_call x1, Pallas kernels, section(): pl.pallas_call(interior_kernel, grid=(count // group,), in_specs=[one_fie...  21 us
    ppermute x3, waiting for transfers between devices, up(): lax.ppermute(value, axis, [(i, i + 1) for i in range(lax.axis_size(axis)...  14.5 us
    ppermute x3, starting transfers between devices, up(): lax.ppermute(value, axis, [(i, i + 1) for i in range(lax.axis_size(axis)...  11.6 us
    ppermute x3, waiting for transfers between devices, down(): lax.ppermute(value, axis, [(i + 1, i) for i in range(lax.axis_size(axis)...  9.3 us
    pallas_call x1, Pallas kernels, section(): pl.pallas_call(functools.partial(combine_kernel, cell_count), grid=(level...  9.2 us
    pallas_call x1, Pallas kernels, section(): pl.pallas_call(layers_kernel, grid=(levels // step,), in_specs=[modes_lev...  4.69 us
    ppermute x3, starting transfers between devices, down(): lax.ppermute(value, axis, [(i + 1, i) for i in range(lax.axis_size(axis)...  4 us
  transfers between devices with their start and end apart: 6, of which 2 were waited for; matrix products, arithmetic and copies ran while one was open for 0% of the time, Pallas kernels for 24%

profile of v1, /device:TPU:0, one launch (start us, length us, event | category | flops | bytes accessed | tf_op | source)
XLA Modules:
  0.0 104.1 jit_solution(2879901565519428831)
XLA Ops:
  0.6 4.7 %shard_map.94 = (f32[16,48,256]{2,1,0:T(8,128)}, f32[16,48,256]{2,1,0:T(8,128)}, f32[6,16,256]{2,1,0:T(8,128)}, f32[4,16,256]{2,1,0:T(8,128)}) custom-call(f32[16,16,16,256]{3,2,1,0:T(8,128)} %modes.7, f32[16,16,256]{2,1,0:T(8,128)} %mean.5, f32[16,16,256]{2,1,0:T(8,128)} %east.3, s32[16,16,256]{2,1,0:T(8,128)} %flag_east.1, s32[16,16,256]{2,1,0:T(8,128)} %mask.5), custom_call_target="tpu_custom_call" | custom-call | tf_op jit(solution)/shard_map/pallas_call | solution.py:433
  5.3 0.0 copy-start.6
  5.3 1.4 %collective-permute-start.5 = (f32[16,48,256]{2,1,0:T(8,128)}, f32[16,48,256]{2,1,0:T(8,128)S(1)}, u32[]{:S(2)}, u32[]{:S(2)}) collective-permute-start(f32[16,48,256]{2,1,0:T(8,128)} %get-tuple-element.28), channel_id=1, source_target_pairs={{4,0},{8,4},{12,8},{16,12},{20,16},{24,20},{28,24},{5,1},{9,5},{13... | collective-permute-start | bytes 2359304 | tf_op jit(solution)/shard_map/ppermute | solution.py:426
  6.7 5.5 %collective-permute-start.4 = (f32[16,48,256]{2,1,0:T(8,128)}, f32[16,48,256]{2,1,0:T(8,128)S(1)}, u32[]{:S(2)}, u32[]{:S(2)}) collective-permute-start(f32[16,48,256]{2,1,0:T(8,128)} %get-tuple-element.23.after_layers), channel_id=1, source_target_pairs={{0,4},{4,8},{8,12},{12,16},{16,20},{20,24},{24,28},{1,5},{5,9},{9,... | collective-permute-start | bytes 2359304 | tf_op jit(solution)/shard_map/ppermute | solution.py:423
  12.3 1.3 %collective-permute-start.1 = (f32[4,16,256]{2,1,0:T(8,128)}, f32[4,16,256]{2,1,0:T(8,128)S(1)}, u32[]{:S(2)}, u32[]{:S(2)}) collective-permute-start(f32[4,16,256]{2,1,0:T(8,128)} %get-tuple-element.22), channel_id=1, source_target_pairs={{4,0},{8,4},{12,8},{16,12},{20,16},{24,20},{28,24},{5,1},{9,5},{13... | collective-permute-start | bytes 196616 | tf_op jit(solution)/shard_map/ppermute | solution.py:426
  13.6 3.8 %shard_map.95 = (f32[16,16,128]{2,1,0:T(8,128)}, f32[16,16,128]{2,1,0:T(8,128)}) custom-call(f32[16,48,256]{2,1,0:T(8,128)} %get-tuple-element.23.after_layers, f32[16,16,16,256]{3,2,1,0:T(8,128)} %modes.7, f32[16,16,256]{2,1,0:T(8,128)} %mean.5, f32[16,16,256]{2,1,0:T(8,128)} %north.3, s32[16,16,256]{2,1,0:T(8,128)} %flag_north.3, s32[16,16,256]{2,1,0:T(8,128)} %mask.5), custom_call_target="tpu_custom_call" | custom-call | tf_op jit(solution)/shard_map/pallas_call | solution.py:449
  17.4 1.5 %collective-permute-start.2 = (f32[16,16,128]{2,1,0:T(8,128)}, f32[16,16,128]{2,1,0:T(8,128)S(1)}, u32[]{:S(2)}, u32[]{:S(2)}) collective-permute-start(f32[16,16,128]{2,1,0:T(8,128)} %get-tuple-element.24), channel_id=1, source_target_pairs={{0,1},{1,2},{2,3},{4,5},{5,6},{6,7},{8,9},{9,10},{10,11},{12,13},{... | collective-permute-start | bytes 393224 | tf_op jit(solution)/shard_map/ppermute | solution.py:423
  18.9 1.3 %collective-permute-start.3 = (f32[16,16,128]{2,1,0:T(8,128)}, f32[16,16,128]{2,1,0:T(8,128)S(1)}, u32[]{:S(2)}, u32[]{:S(2)}) collective-permute-start(f32[16,16,128]{2,1,0:T(8,128)} %get-tuple-element.25), channel_id=1, source_target_pairs={{1,0},{2,1},{3,2},{5,4},{6,5},{7,6},{9,8},{10,9},{11,10},{13,12},{... | collective-permute-start | bytes 393224 | tf_op jit(solution)/shard_map/ppermute | solution.py:426
  20.2 9.3 %collective-permute-done.1.side_after = f32[4,16,256]{2,1,0:T(8,128)S(1)} collective-permute-done((f32[4,16,256]{2,1,0:T(8,128)}, f32[4,16,256]{2,1,0:T(8,128)S(1)}, u32[]{:S(2)}, u32[]{:S(2)}) %collective-permute-start.1) | collective-permute-done | bytes 65568 | tf_op jit(solution)/shard_map/ppermute | solution.py:426
  29.5 0.0 copy-start.5
  29.5 0.0 copy-done.6
  29.5 4.6 %collective-permute-start = (f32[6,16,256]{2,1,0:T(8,128)S(1)}, f32[6,16,256]{2,1,0:T(8,128)S(1)}, u32[]{:S(2)}, u32[]{:S(2)}) collective-permute-start(f32[6,16,256]{2,1,0:T(8,128)S(1)} %copy-done.6), channel_id=1, source_target_pairs={{0,4},{4,8},{8,12},{12,16},{16,20},{20,24},{24,28},{1,5},{5,9},{9,... | collective-permute-start | bytes 294920 | tf_op jit(solution)/shard_map/ppermute | solution.py:423
  34.1 14.5 %collective-permute-done.side_before = f32[6,16,256]{2,1,0:T(8,128)S(1)} collective-permute-done((f32[6,16,256]{2,1,0:T(8,128)S(1)}, f32[6,16,256]{2,1,0:T(8,128)S(1)}, u32[]{:S(2)}, u32[]{:S(2)}) %collective-permute-start) | collective-permute-done | bytes 98336 | tf_op jit(solution)/shard_map/ppermute | solution.py:423
  48.6 0.0 copy-start.4
  48.6 0.0 collective-permute-done.2.before
  48.6 0.0 copy-start.2
  48.6 0.0 collective-permute-done.3.after
  48.6 0.0 copy-done.5
  48.6 0.6 copy-done.4
  49.2 0.0 copy-done.2
  49.3 0.0 copy-start.3
  49.3 0.6 copy-done.3
  49.9 21.0 %shard_map.96 = (f32[16,16,16,256]{3,2,1,0:T(8,128)}, f32[16,16,256]{2,1,0:T(8,128)}, f32[16,8,256]{2,1,0:T(8,128)}, f32[16,8,256]{2,1,0:T(8,128)}, f32[16,8,256...) custom-call(f32[16,16,16,256]{3,2,1,0:T(8,128)} %modes.7, ...), custom_call_target="tpu_custom_call" | custom-call | flops 62914560 | bytes 12582912 | tf_op jit(solution)/shard_map/pallas_call | solution.py:465
  70.9 0.0 collective-permute-done.5.high
  70.9 0.0 copy-start
  71.0 0.0 collective-permute-done.4.low
  71.0 0.0 copy-start.1
  71.0 0.9 copy-done
  71.8 0.3 copy-done.1
  72.1 22.8 %shard_map.97 = (f32[16,16,16,256]{3,2,1,0:T(8,128)}, f32[8,128]{1,0:T(8,128)}) custom-call(f32[16,16,16,256]{3,2,1,0:T(8,128)} %modes.7, f32[16,16,16,256]{3,2,1,0:T(8,128)} %get-tuple-element.27.partial, f32[16,48,256]{2,1,0:T(8,128)} %copy-done.1, f32[16,48,256]{2,1,0:T(8,128)} %copy-done, f32[16,8,256]{2,1,0:T(8,128)} %get-tuple-element.29.l3, ...), custom_call_target="tpu_custom_call" | custom-call | tf_op jit(solution)/shard_map/pallas_call | solution.py:485
  94.9 9.2 %shard_map.98 = (f32[16,16,16,256]{3,2,1,0:T(8,128)}, f32[16,16]{1,0:T(8,128)}) custom-call(f32[8,128]{1,0:T(8,128)} %get-tuple-element.35.packed, f32[16,16,16,256]{3,2,1,0:T(8,128)} %modes.7, f32[16,16,16,256]{3,2,1,0:T(8,128)} %get-tuple-element.36.tend), custom_call_target="tpu_custom_call" | custom-call | tf_op jit(solution)/shard_map/pallas_call | solution.py:507
Async XLA Ops:
  5.3 24.1 %copy-start.6 = (f32[6,16,256]{2,1,0:T(8,128)S(1)}, f32[6,16,256]{2,1,0:T(8,128)}, u32[]{:S(2)}) copy-start(f32[6,16,256]{2,1,0:T(8,128)} %get-tuple-element.21) | copy-start | bytes 294916
  5.3 65.6 %collective-permute-start.5 = (f32[16,48,256]{2,1,0:T(8,128)}, f32[16,48,256]{2,1,0:T(8,128)S(1)}, u32[]{:S(2)}, u32[]{:S(2)}) collective-permute-start(f32[16,48,256]{2,1,0:T(8,128)} %get-tuple-element.28), channel_id=1, source_target_pairs={{4,0},{8,4},{12,8},{16,12},{20,16},{24,20},{28,24},{5,1},{9,5},{13... | collective-permute-start | bytes 2359304 | tf_op jit(solution)/shard_map/ppermute | solution.py:426
  6.7 64.2 %collective-permute-start.4 = (f32[16,48,256]{2,1,0:T(8,128)}, f32[16,48,256]{2,1,0:T(8,128)S(1)}, u32[]{:S(2)}, u32[]{:S(2)}) collective-permute-start(f32[16,48,256]{2,1,0:T(8,128)} %get-tuple-element.23.after_layers), channel_id=1, source_target_pairs={{0,4},{4,8},{8,12},{12,16},{16,20},{20,24},{24,28},{1,5},{5,9},{9,... | collective-permute-start | bytes 2359304 | tf_op jit(solution)/shard_map/ppermute | solution.py:423
  12.3 17.2 %collective-permute-start.1 = (f32[4,16,256]{2,1,0:T(8,128)}, f32[4,16,256]{2,1,0:T(8,128)S(1)}, u32[]{:S(2)}, u32[]{:S(2)}) collective-permute-start(f32[4,16,256]{2,1,0:T(8,128)} %get-tuple-element.22), channel_id=1, source_target_pairs={{4,0},{8,4},{12,8},{16,12},{20,16},{24,20},{28,24},{5,1},{9,5},{13... | collective-permute-start | bytes 196616 | tf_op jit(solution)/shard_map/ppermute | solution.py:426
  17.4 31.2 %collective-permute-start.2 = (f32[16,16,128]{2,1,0:T(8,128)}, f32[16,16,128]{2,1,0:T(8,128)S(1)}, u32[]{:S(2)}, u32[]{:S(2)}) collective-permute-start(f32[16,16,128]{2,1,0:T(8,128)} %get-tuple-element.24), channel_id=1, source_target_pairs={{0,1},{1,2},{2,3},{4,5},{5,6},{6,7},{8,9},{9,10},{10,11},{12,13},{... | collective-permute-start | bytes 393224 | tf_op jit(solution)/shard_map/ppermute | solution.py:423
  18.9 29.7 %collective-permute-start.3 = (f32[16,16,128]{2,1,0:T(8,128)}, f32[16,16,128]{2,1,0:T(8,128)S(1)}, u32[]{:S(2)}, u32[]{:S(2)}) collective-permute-start(f32[16,16,128]{2,1,0:T(8,128)} %get-tuple-element.25), channel_id=1, source_target_pairs={{1,0},{2,1},{3,2},{5,4},{6,5},{7,6},{9,8},{10,9},{11,10},{13,12},{... | collective-permute-start | bytes 393224 | tf_op jit(solution)/shard_map/ppermute | solution.py:426
  29.5 19.1 %copy-start.5 = (f32[4,16,256]{2,1,0:T(8,128)}, f32[4,16,256]{2,1,0:T(8,128)S(1)}, u32[]{:S(2)}) copy-start(f32[4,16,256]{2,1,0:T(8,128)S(1)} %collective-permute-done.1.side_after) | copy-start | bytes 196612
  29.5 19.1 %collective-permute-start = (f32[6,16,256]{2,1,0:T(8,128)S(1)}, f32[6,16,256]{2,1,0:T(8,128)S(1)}, u32[]{:S(2)}, u32[]{:S(2)}) collective-permute-start(f32[6,16,256]{2,1,0:T(8,128)S(1)} %copy-done.6), channel_id=1, source_target_pairs={{0,4},{4,8},{8,12},{12,16},{16,20},{20,24},{24,28},{1,5},{5,9},{9,... | collective-permute-start | bytes 294920 | tf_op jit(solution)/shard_map/ppermute | solution.py:423
  48.6 0.6 copy-start.4
  48.6 0.7 copy-start.2
  49.3 0.6 copy-start.3
  70.9 0.9 copy-start
  71.0 1.2 %copy-start.1 = (f32[16,48,256]{2,1,0:T(8,128)}, f32[16,48,256]{2,1,0:T(8,128)S(1)}, u32[]{:S(2)}) copy-start(f32[16,48,256]{2,1,0:T(8,128)S(1)} %collective-permute-done.4.low) | copy-start | bytes 2359300

commit v2 on v1

--- a/solution.py
+++ b/solution.py
@@ -376,23 +376,20 @@
         spread = (
             lax.broadcasted_iota(jnp.int32, (tall, count), 0) // SUB
             == lax.broadcasted_iota(jnp.int32, (tall, count), 1)
-        ).astype(jnp.float32)
+        ).astype(jnp.bfloat16)
         along = (
             lax.broadcasted_iota(jnp.int32, (2 * count, wide), 1) // SUB
             == lax.broadcasted_iota(jnp.int32, (2 * count, wide), 0)
-        ).astype(jnp.float32)
-        whole = jnp.dot(
-            jnp.dot(spread, mix, precision=HIGHEST, preferred_element_type=jnp.float32),
-            along,
-            precision=HIGHEST,
-            preferred_element_type=jnp.float32,
-        )
+        ).astype(jnp.bfloat16)
         row = lax.broadcasted_iota(jnp.int32, (tall, wide), 0)
         col = lax.broadcasted_iota(jnp.int32, (tall, wide), 1)
-        whole = jnp.where((row % SUB) == (col % SUB), whole, 0.0)
-        coarse = whole.astype(jnp.bfloat16)
-        weights[:tall, :] = coarse
-        weights[tall:, :] = (whole - coarse.astype(jnp.float32)).astype(jnp.bfloat16)
+        kept = (row % SUB) == (col % SUB)
+        coarse = mix.astype(jnp.bfloat16)
+        fine = (mix - coarse.astype(jnp.float32)).astype(jnp.bfloat16)
+        for place, value in ((0, coarse), (tall, fine)):
+            taller = jnp.dot(spread, value, preferred_element_type=jnp.float32).astype(jnp.bfloat16)
+            whole = jnp.dot(taller, along, preferred_element_type=jnp.float32)
+            weights[place : place + tall, :] = jnp.where(kept, whole, 0.0).astype(jnp.bfloat16)
 
     for k in range(levels):
         for part in range(size_x // SUB):
@@ -504,11 +501,13 @@
     )(mode_fields, partial, x_before, x_after, *outer)
 
     cell_count = float(levels * size_x * size_y * nx * ny)
+    small = divisor(levels, 2)
+    few_levels = pl.BlockSpec((count, small, size_x, size_y), lambda z: (0, z, 0, 0))
     modes_next, factor = pl.pallas_call(
         functools.partial(combine_kernel, cell_count),
-        grid=(levels // step,),
-        in_specs=[pl.BlockSpec(packed, lambda z: (0, 0)), modes_level, modes_level],
-        out_specs=[modes_level, pl.BlockSpec((count, count), lambda z: (0, 0))],
+        grid=(levels // small,),
+        in_specs=[pl.BlockSpec(packed, lambda z: (0, 0)), few_levels, few_levels],
+        out_specs=[few_levels, pl.BlockSpec((count, count), lambda z: (0, 0))],
         out_shape=[jax.ShapeDtypeStruct(mode_fields.shape, f32), jax.ShapeDtypeStruct((count, count), f32)],
         scratch_shapes=[pltpu.VMEM((wide, wide), jnp.bfloat16)],
     )(gram, mode_fields, tend)

time: 105 us -> 107 us (1.019)
  Pallas kernels: 61.5 us -> 63.4 us
    pallas_call x1, Pallas kernels: 9.2 us -> 11.1 us  [section(): pl.pallas_call(functools.partial(combine_kernel, cell_count), grid=(level...]
  transfers between devices with their start and end apart: 6 -> 6, of which waited for: 2 -> 2; matrix products, arithmetic and copies ran while one was open for 0% -> 0% of each run, Pallas kernels for 24% -> 23%
where the time goes in v2:
time: 107 us; the launch traced here: 106 us
  Pallas kernels  63.4 us (59%)
  waiting for transfers between devices  23.8 us (22%)
  starting transfers between devices  15.6 us (15%)
  local copies, waits for them, and re-layouts  2.47 us (2%)
    pallas_call x1, Pallas kernels, section(): pl.pallas_call(functools.partial(gram_kernel, nx, ny), grid=(levels // st...  22.8 us
    pallas_call x1, Pallas kernels, section(): pl.pallas_call(interior_kernel, grid=(count // group,), in_specs=[one_fie...  21 us
    ppermute x3, waiting for transfers between devices, up(): lax.ppermute(value, axis, [(i, i + 1) for i in range(lax.axis_size(axis)...  14.5 us
    ppermute x3, starting transfers between devices, up(): lax.ppermute(value, axis, [(i, i + 1) for i in range(lax.axis_size(axis)...  11.6 us
    pallas_call x1, Pallas kernels, section(): pl.pallas_call(functools.partial(combine_kernel, cell_count), grid=(level...  11.1 us
    ppermute x3, waiting for transfers between devices, down(): lax.ppermute(value, axis, [(i + 1, i) for i in range(lax.axis_size(axis)...  9.3 us
    pallas_call x1, Pallas kernels, section(): pl.pallas_call(layers_kernel, grid=(levels // step,), in_specs=[modes_lev...  4.69 us
    ppermute x3, starting transfers between devices, down(): lax.ppermute(value, axis, [(i + 1, i) for i in range(lax.axis_size(axis)...  4 us
  transfers between devices with their start and end apart: 6, of which 2 were waited for; matrix products, arithmetic and copies ran while one was open for 0% of the time, Pallas kernels for 23%

profile of v2, /device:TPU:0, one launch (start us, length us, event | category | flops | bytes accessed | tf_op | source)
XLA Modules:
  0.0 106.0 jit_solution(9940483864746008)
XLA Ops:
  0.6 4.7 %shard_map.94 = (f32[16,48,256]{2,1,0:T(8,128)}, f32[16,48,256]{2,1,0:T(8,128)}, f32[6,16,256]{2,1,0:T(8,128)}, f32[4,16,256]{2,1,0:T(8,128)}) custom-call(f32[16,16,16,256]{3,2,1,0:T(8,128)} %modes.7, f32[16,16,256]{2,1,0:T(8,128)} %mean.5, f32[16,16,256]{2,1,0:T(8,128)} %east.3, s32[16,16,256]{2,1,0:T(8,128)} %flag_east.1, s32[16,16,256]{2,1,0:T(8,128)} %mask.5), custom_call_target="tpu_custom_call" | custom-call | tf_op jit(solution)/shard_map/pallas_call | solution.py:430
  5.3 0.0 copy-start.6
  5.3 1.4 %collective-permute-start.5 = (f32[16,48,256]{2,1,0:T(8,128)}, f32[16,48,256]{2,1,0:T(8,128)S(1)}, u32[]{:S(2)}, u32[]{:S(2)}) collective-permute-start(f32[16,48,256]{2,1,0:T(8,128)} %get-tuple-element.28), channel_id=1, source_target_pairs={{4,0},{8,4},{12,8},{16,12},{20,16},{24,20},{28,24},{5,1},{9,5},{13... | collective-permute-start | bytes 2359304 | tf_op jit(solution)/shard_map/ppermute | solution.py:423
  6.7 5.5 %collective-permute-start.4 = (f32[16,48,256]{2,1,0:T(8,128)}, f32[16,48,256]{2,1,0:T(8,128)S(1)}, u32[]{:S(2)}, u32[]{:S(2)}) collective-permute-start(f32[16,48,256]{2,1,0:T(8,128)} %get-tuple-element.23.after_layers), channel_id=1, source_target_pairs={{0,4},{4,8},{8,12},{12,16},{16,20},{20,24},{24,28},{1,5},{5,9},{9,... | collective-permute-start | bytes 2359304 | tf_op jit(solution)/shard_map/ppermute | solution.py:420
  12.3 1.3 %collective-permute-start.1 = (f32[4,16,256]{2,1,0:T(8,128)}, f32[4,16,256]{2,1,0:T(8,128)S(1)}, u32[]{:S(2)}, u32[]{:S(2)}) collective-permute-start(f32[4,16,256]{2,1,0:T(8,128)} %get-tuple-element.22), channel_id=1, source_target_pairs={{4,0},{8,4},{12,8},{16,12},{20,16},{24,20},{28,24},{5,1},{9,5},{13... | collective-permute-start | bytes 196616 | tf_op jit(solution)/shard_map/ppermute | solution.py:423
  13.6 3.8 %shard_map.95 = (f32[16,16,128]{2,1,0:T(8,128)}, f32[16,16,128]{2,1,0:T(8,128)}) custom-call(f32[16,48,256]{2,1,0:T(8,128)} %get-tuple-element.23.after_layers, f32[16,16,16,256]{3,2,1,0:T(8,128)} %modes.7, f32[16,16,256]{2,1,0:T(8,128)} %mean.5, f32[16,16,256]{2,1,0:T(8,128)} %north.3, s32[16,16,256]{2,1,0:T(8,128)} %flag_north.3, s32[16,16,256]{2,1,0:T(8,128)} %mask.5), custom_call_target="tpu_custom_call" | custom-call | tf_op jit(solution)/shard_map/pallas_call | solution.py:446
  17.4 1.5 %collective-permute-start.2 = (f32[16,16,128]{2,1,0:T(8,128)}, f32[16,16,128]{2,1,0:T(8,128)S(1)}, u32[]{:S(2)}, u32[]{:S(2)}) collective-permute-start(f32[16,16,128]{2,1,0:T(8,128)} %get-tuple-element.24), channel_id=1, source_target_pairs={{0,1},{1,2},{2,3},{4,5},{5,6},{6,7},{8,9},{9,10},{10,11},{12,13},{... | collective-permute-start | bytes 393224 | tf_op jit(solution)/shard_map/ppermute | solution.py:420
  18.9 1.3 %collective-permute-start.3 = (f32[16,16,128]{2,1,0:T(8,128)}, f32[16,16,128]{2,1,0:T(8,128)S(1)}, u32[]{:S(2)}, u32[]{:S(2)}) collective-permute-start(f32[16,16,128]{2,1,0:T(8,128)} %get-tuple-element.25), channel_id=1, source_target_pairs={{1,0},{2,1},{3,2},{5,4},{6,5},{7,6},{9,8},{10,9},{11,10},{13,12},{... | collective-permute-start | bytes 393224 | tf_op jit(solution)/shard_map/ppermute | solution.py:423
  20.2 9.3 %collective-permute-done.1.side_after = f32[4,16,256]{2,1,0:T(8,128)S(1)} collective-permute-done((f32[4,16,256]{2,1,0:T(8,128)}, f32[4,16,256]{2,1,0:T(8,128)S(1)}, u32[]{:S(2)}, u32[]{:S(2)}) %collective-permute-start.1) | collective-permute-done | bytes 65568 | tf_op jit(solution)/shard_map/ppermute | solution.py:423
  29.5 0.0 copy-start.5
  29.5 0.0 copy-done.6
  29.5 4.6 %collective-permute-start = (f32[6,16,256]{2,1,0:T(8,128)S(1)}, f32[6,16,256]{2,1,0:T(8,128)S(1)}, u32[]{:S(2)}, u32[]{:S(2)}) collective-permute-start(f32[6,16,256]{2,1,0:T(8,128)S(1)} %copy-done.6), channel_id=1, source_target_pairs={{0,4},{4,8},{8,12},{12,16},{16,20},{20,24},{24,28},{1,5},{5,9},{9,... | collective-permute-start | bytes 294920 | tf_op jit(solution)/shard_map/ppermute | solution.py:420
  34.1 14.5 %collective-permute-done.side_before = f32[6,16,256]{2,1,0:T(8,128)S(1)} collective-permute-done((f32[6,16,256]{2,1,0:T(8,128)S(1)}, f32[6,16,256]{2,1,0:T(8,128)S(1)}, u32[]{:S(2)}, u32[]{:S(2)}) %collective-permute-start) | collective-permute-done | bytes 98336 | tf_op jit(solution)/shard_map/ppermute | solution.py:420
  48.6 0.0 copy-start.4
  48.6 0.0 collective-permute-done.2.before
  48.6 0.0 copy-start.2
  48.6 0.0 collective-permute-done.3.after
  48.6 0.0 copy-done.5
  48.6 0.6 copy-done.4
  49.2 0.0 copy-done.2
  49.3 0.0 copy-start.3
  49.3 0.6 copy-done.3
  49.9 21.0 %shard_map.96 = (f32[16,16,16,256]{3,2,1,0:T(8,128)}, f32[16,16,256]{2,1,0:T(8,128)}, f32[16,8,256]{2,1,0:T(8,128)}, f32[16,8,256]{2,1,0:T(8,128)}, f32[16,8,256...) custom-call(f32[16,16,16,256]{3,2,1,0:T(8,128)} %modes.7, ...), custom_call_target="tpu_custom_call" | custom-call | flops 62914560 | bytes 12582912 | tf_op jit(solution)/shard_map/pallas_call | solution.py:462
  70.9 0.0 collective-permute-done.5.high
  70.9 0.0 copy-start
  71.0 0.0 collective-permute-done.4.low
  71.0 0.0 copy-start.1
  71.0 0.9 copy-done
  71.8 0.3 copy-done.1
  72.1 22.8 %shard_map.97 = (f32[16,16,16,256]{3,2,1,0:T(8,128)}, f32[8,128]{1,0:T(8,128)}) custom-call(f32[16,16,16,256]{3,2,1,0:T(8,128)} %modes.7, f32[16,16,16,256]{3,2,1,0:T(8,128)} %get-tuple-element.27.partial, f32[16,48,256]{2,1,0:T(8,128)} %copy-done.1, f32[16,48,256]{2,1,0:T(8,128)} %copy-done, f32[16,8,256]{2,1,0:T(8,128)} %get-tuple-element.29.l3, ...), custom_call_target="tpu_custom_call" | custom-call | tf_op jit(solution)/shard_map/pallas_call | solution.py:482
  94.9 11.1 %shard_map.98 = (f32[16,16,16,256]{3,2,1,0:T(8,128)}, f32[16,16]{1,0:T(8,128)}) custom-call(f32[8,128]{1,0:T(8,128)} %get-tuple-element.35.packed, f32[16,16,16,256]{3,2,1,0:T(8,128)} %modes.7, f32[16,16,16,256]{3,2,1,0:T(8,128)} %get-tuple-element.36.tend), custom_call_target="tpu_custom_call" | custom-call | tf_op jit(solution)/shard_map/pallas_call | solution.py:506
Async XLA Ops:
  5.3 24.1 %copy-start.6 = (f32[6,16,256]{2,1,0:T(8,128)S(1)}, f32[6,16,256]{2,1,0:T(8,128)}, u32[]{:S(2)}) copy-start(f32[6,16,256]{2,1,0:T(8,128)} %get-tuple-element.21) | copy-start | bytes 294916
  5.3 65.6 %collective-permute-start.5 = (f32[16,48,256]{2,1,0:T(8,128)}, f32[16,48,256]{2,1,0:T(8,128)S(1)}, u32[]{:S(2)}, u32[]{:S(2)}) collective-permute-start(f32[16,48,256]{2,1,0:T(8,128)} %get-tuple-element.28), channel_id=1, source_target_pairs={{4,0},{8,4},{12,8},{16,12},{20,16},{24,20},{28,24},{5,1},{9,5},{13... | collective-permute-start | bytes 2359304 | tf_op jit(solution)/shard_map/ppermute | solution.py:423
  6.7 64.2 %collective-permute-start.4 = (f32[16,48,256]{2,1,0:T(8,128)}, f32[16,48,256]{2,1,0:T(8,128)S(1)}, u32[]{:S(2)}, u32[]{:S(2)}) collective-permute-start(f32[16,48,256]{2,1,0:T(8,128)} %get-tuple-element.23.after_layers), channel_id=1, source_target_pairs={{0,4},{4,8},{8,12},{12,16},{16,20},{20,24},{24,28},{1,5},{5,9},{9,... | collective-permute-start | bytes 2359304 | tf_op jit(solution)/shard_map/ppermute | solution.py:420
  12.3 17.2 %collective-permute-start.1 = (f32[4,16,256]{2,1,0:T(8,128)}, f32[4,16,256]{2,1,0:T(8,128)S(1)}, u32[]{:S(2)}, u32[]{:S(2)}) collective-permute-start(f32[4,16,256]{2,1,0:T(8,128)} %get-tuple-element.22), channel_id=1, source_target_pairs={{4,0},{8,4},{12,8},{16,12},{20,16},{24,20},{28,24},{5,1},{9,5},{13... | collective-permute-start | bytes 196616 | tf_op jit(solution)/shard_map/ppermute | solution.py:423
  17.4 31.2 %collective-permute-start.2 = (f32[16,16,128]{2,1,0:T(8,128)}, f32[16,16,128]{2,1,0:T(8,128)S(1)}, u32[]{:S(2)}, u32[]{:S(2)}) collective-permute-start(f32[16,16,128]{2,1,0:T(8,128)} %get-tuple-element.24), channel_id=1, source_target_pairs={{0,1},{1,2},{2,3},{4,5},{5,6},{6,7},{8,9},{9,10},{10,11},{12,13},{... | collective-permute-start | bytes 393224 | tf_op jit(solution)/shard_map/ppermute | solution.py:420
  18.9 29.7 %collective-permute-start.3 = (f32[16,16,128]{2,1,0:T(8,128)}, f32[16,16,128]{2,1,0:T(8,128)S(1)}, u32[]{:S(2)}, u32[]{:S(2)}) collective-permute-start(f32[16,16,128]{2,1,0:T(8,128)} %get-tuple-element.25), channel_id=1, source_target_pairs={{1,0},{2,1},{3,2},{5,4},{6,5},{7,6},{9,8},{10,9},{11,10},{13,12},{... | collective-permute-start | bytes 393224 | tf_op jit(solution)/shard_map/ppermute | solution.py:423
  29.5 19.1 %copy-start.5 = (f32[4,16,256]{2,1,0:T(8,128)}, f32[4,16,256]{2,1,0:T(8,128)S(1)}, u32[]{:S(2)}) copy-start(f32[4,16,256]{2,1,0:T(8,128)S(1)} %collective-permute-done.1.side_after) | copy-start | bytes 196612
  29.5 19.1 %collective-permute-start = (f32[6,16,256]{2,1,0:T(8,128)S(1)}, f32[6,16,256]{2,1,0:T(8,128)S(1)}, u32[]{:S(2)}, u32[]{:S(2)}) collective-permute-start(f32[6,16,256]{2,1,0:T(8,128)S(1)} %copy-done.6), channel_id=1, source_target_pairs={{0,4},{4,8},{8,12},{12,16},{16,20},{20,24},{24,28},{1,5},{5,9},{9,... | collective-permute-start | bytes 294920 | tf_op jit(solution)/shard_map/ppermute | solution.py:420
  48.6 0.6 copy-start.4
  48.6 0.7 copy-start.2
  49.3 0.6 copy-start.3
  70.9 0.9 copy-start
  71.0 1.2 %copy-start.1 = (f32[16,48,256]{2,1,0:T(8,128)}, f32[16,48,256]{2,1,0:T(8,128)S(1)}, u32[]{:S(2)}) copy-start(f32[16,48,256]{2,1,0:T(8,128)S(1)} %collective-permute-done.4.low) | copy-start | bytes 2359300
